TPU v7x, 32 devices: a whole 2x2x4 slice. The times are simulated.
32 devices in a mesh: batch: 4 (over y, x), ctx: 8 (over z, core).
Axes of the slice: x: 2, y: 2, z: 4, core: 2. Of those that a mesh axis runs over, the one named last changes fastest.
Arguments:
- inputs: float32 [4, 1024, 2304], P('batch', 'ctx'), may hold values from -6 to 6
- block_order: int32 [4, 8], P('batch'), may hold values from 0 to 7, each once within a row
- cotangent: float32 [4, 1024, 2304], P('batch', 'ctx'), may hold values from -6 to 6
- attn_gain: bfloat16 [2304], P(('batch', 'ctx')), may hold values from 0.5 to 1.5
- post_attn_gain: bfloat16 [2304], P(('batch', 'ctx')), may hold values from 0.5 to 1.5
- ffn_gain: bfloat16 [2304], P(('batch', 'ctx')), may hold values from 0.5 to 1.5
- post_ffn_gain: bfloat16 [2304], P(('batch', 'ctx')), may hold values from 0.5 to 1.5
- query_weight: bfloat16 [2304, 2048], P(('batch', 'ctx')), may hold values from -0.5 to 0.5
- key_weight: bfloat16 [2304, 1024], P(('batch', 'ctx')), may hold values from -0.125 to 0.125
- value_weight: bfloat16 [2304, 1024], P(('batch', 'ctx')), may hold values from -0.125 to 0.125
- out_weight: bfloat16 [2048, 2304], P(('batch', 'ctx')), may hold values from -0.125 to 0.125
- gate_weight: bfloat16 [9216, 2304], P(('batch', 'ctx')), may hold values from -0.125 to 0.125
- up_weight: bfloat16 [9216, 2304], P(('batch', 'ctx')), may hold values from -0.125 to 0.125
- down_weight: bfloat16 [9216, 2304], P(('batch', 'ctx')), may hold values from -0.0625 to 0.0625
Outputs:
- output: float32 [4, 1024, 2304], P('batch', 'ctx')
- input_grad: float32 [4, 1024, 2304], P('batch', 'ctx')
- query_grad: float32 [2304, 2048], P(('batch', 'ctx'))
- key_grad: float32 [2304, 1024], P(('batch', 'ctx'))
- value_grad: float32 [2304, 1024], P(('batch', 'ctx'))
- out_grad: float32 [2048, 2304], P(('batch', 'ctx'))
- gate_grad: float32 [9216, 2304], P(('batch', 'ctx'))
- up_grad: float32 [9216, 2304], P(('batch', 'ctx'))
- down_grad: float32 [9216, 2304], P(('batch', 'ctx'))
- attn_gain_grad: float32 [2304], P(('batch', 'ctx'))
- post_attn_gain_grad: float32 [2304], P(('batch', 'ctx'))
- ffn_gain_grad: float32 [2304], P(('batch', 'ctx'))
- post_ffn_gain_grad: float32 [2304], P(('batch', 'ctx'))
Inputs may be any that keep to these rules, and one draw needn't show every extreme that they name: Each row of block_order names every block of 128 positions of its sequence exactly once.
All inputs are finite; a program needn't handle non-finite values.
Results may differ from a plain program's by a relative error of at most 0.02.
The roundings to bfloat16 on the way count: a program that leaves them out, or rounds other values in their place, can miss the bound.
Values may be sent and summed in bfloat16 or wider, within the bound.
No kernel may reach another device: no remote copies, remote signals or barrier semaphores. Data moves between devices by JAX's collectives and lax.ppermute only.
A program may use at most 512 MiB of HBM per device.

v0:
```python
import math
import jax
import jax.numpy as jnp
from jax import lax
from jax.sharding import PartitionSpec as P

HEADS = 8
KV_HEADS = 4
HEAD_DIM = 256
NORM_EPS = 1e-06
SOFT_CAP = 50.0


def normalize(values_in, gain_vec):
    inv_rms = lax.rsqrt(jnp.mean(values_in * values_in, axis=-1, keepdims=True) + NORM_EPS)
    return (values_in * inv_rms * gain_vec.astype(jnp.float32), inv_rms)


def norm_back(values_in, inv_rms, gain_vec, grad_in):
    scaled = values_in * inv_rms
    weighted = grad_in * gain_vec.astype(jnp.float32)
    grad_gain = jnp.sum(grad_in * scaled, axis=0)
    grad_values = inv_rms * (
        weighted - scaled * jnp.mean(weighted * scaled, axis=-1, keepdims=True)
    )
    return (grad_values, grad_gain)


def geglu(gate_val, up_val):
    return jax.nn.gelu(gate_val, approximate=True) * up_val


def rows_product(left_mat, right_mat):
    return lax.dot_general(
        left_mat, right_mat, (((1,), (1,)), ((), ())), preferred_element_type=jnp.float32
    )


def cols_product(left_mat, right_mat):
    return lax.dot_general(
        left_mat, right_mat, (((0,), (0,)), ((), ())), preferred_element_type=jnp.float32
    )


def key_positions(block_row, row_count, local_rows):
    row_index = jnp.arange(row_count, dtype=jnp.int32)
    which_block = row_index // local_rows
    block_ids = jnp.arange(block_row.shape[0], dtype=jnp.int32)
    matches = which_block[:, None] == block_ids[None, :]
    chosen = jnp.sum(jnp.where(matches, block_row[None, :], 0), axis=1)
    return chosen * local_rows + row_index % local_rows


def on_device(
    inputs,
    block_order,
    cotangent,
    attn_gain,
    post_attn_gain,
    ffn_gain,
    post_ffn_gain,
    query_weight,
    key_weight,
    value_weight,
    out_weight,
    gate_weight,
    up_weight,
    down_weight,
):
    local_rows = inputs.shape[1]
    features = inputs.shape[2]
    rows_x = inputs.reshape(local_rows, features)
    grad_y = cotangent.reshape(local_rows, features)
    block_row = block_order.reshape(-1)
    block_count = block_row.shape[0]
    seq_length = local_rows * block_count
    groups = KV_HEADS
    ratio = HEADS // KV_HEADS
    key_width = KV_HEADS * HEAD_DIM
    scale = 1.0 / math.sqrt(HEAD_DIM)
    ctx_index = lax.axis_index("ctx")
    own_block = jnp.sum(
        jnp.where(jnp.arange(block_count, dtype=jnp.int32) == ctx_index, block_row, 0)
    )
    query_pos = own_block * local_rows + jnp.arange(local_rows, dtype=jnp.int32)
    gathered = (
        lax.all_gather(query_weight, ("batch", "ctx"), axis=0, tiled=True),
        lax.all_gather(key_weight, ("batch", "ctx"), axis=0, tiled=True),
        lax.all_gather(value_weight, ("batch", "ctx"), axis=0, tiled=True),
        lax.all_gather(out_weight, ("batch", "ctx"), axis=0, tiled=True),
        lax.all_gather(attn_gain, ("batch", "ctx"), axis=0, tiled=True),
        lax.all_gather(post_attn_gain, ("batch", "ctx"), axis=0, tiled=True),
        lax.all_gather(ffn_gain, ("batch", "ctx"), axis=0, tiled=True),
        lax.all_gather(post_ffn_gain, ("batch", "ctx"), axis=0, tiled=True),
    )
    w_query, w_key, w_value, w_out, gain_one, gain_two, gain_three, gain_four = gathered
    normed, inv_one = normalize(rows_x, gain_one)
    normed_in = normed.astype(jnp.bfloat16)
    query = jnp.dot(normed_in, w_query, preferred_element_type=jnp.float32).astype(jnp.bfloat16)
    kv_local = jnp.concatenate(
        (
            jnp.dot(normed_in, w_key, preferred_element_type=jnp.float32),
            jnp.dot(normed_in, w_value, preferred_element_type=jnp.float32),
        ),
        axis=1,
    ).astype(jnp.bfloat16)
    q_heads = query.reshape(local_rows, groups, ratio, HEAD_DIM)
    shard_piece = lax.all_gather(kv_local, "ctx", axis=0, tiled=True)
    row_count = shard_piece.shape[0]
    key_heads = shard_piece[:, :key_width].reshape(row_count, groups, HEAD_DIM)
    value_heads = shard_piece[:, key_width:].reshape(row_count, groups, HEAD_DIM)
    key_pos = key_positions(block_row, row_count, local_rows)
    visible = key_pos[None, :] <= query_pos[:, None]
    tanh_val = jnp.tanh(
        jnp.einsum("tgrd,jgd->grtj", q_heads, key_heads, preferred_element_type=jnp.float32)
        * scale
        / SOFT_CAP
    )
    raw = jnp.where(visible, jnp.exp(SOFT_CAP * tanh_val), 0.0)
    accum = jnp.einsum(
        "grtj,jgd->tgrd", raw.astype(jnp.bfloat16), value_heads, preferred_element_type=jnp.float32
    )
    totals = jnp.sum(raw, axis=3)
    accum, totals, kv_all = (accum, totals, shard_piece)
    attended = (
        (accum / jnp.transpose(totals, (2, 0, 1))[..., None])
        .reshape(local_rows, HEADS * HEAD_DIM)
        .astype(jnp.bfloat16)
    )
    branch = jnp.dot(attended, w_out, preferred_element_type=jnp.float32)
    branch_normed, inv_two = normalize(branch, gain_two)
    middle = rows_x + branch_normed
    normed_m, inv_three = normalize(middle, gain_three)
    normed_mid = normed_m.astype(jnp.bfloat16)
    gate_piece = lax.all_gather(gate_weight, ("batch", "ctx"), axis=0, tiled=True)
    up_piece = lax.all_gather(up_weight, ("batch", "ctx"), axis=0, tiled=True)
    down_piece = lax.all_gather(down_weight, ("batch", "ctx"), axis=0, tiled=True)
    hidden_piece = geglu(
        rows_product(normed_mid, gate_piece), rows_product(normed_mid, up_piece)
    ).astype(jnp.bfloat16)
    ffn_out = jnp.dot(hidden_piece, down_piece, preferred_element_type=jnp.float32)
    ffn_normed, inv_four = normalize(ffn_out, gain_four)
    output = middle + ffn_normed
    grad_ffn, grad_four = norm_back(ffn_out, inv_four, gain_four, grad_y)
    grad_ffn_b = grad_ffn.astype(jnp.bfloat16)
    gate_piece = lax.all_gather(gate_weight, ("batch", "ctx"), axis=0, tiled=True)
    up_piece = lax.all_gather(up_weight, ("batch", "ctx"), axis=0, tiled=True)
    down_piece = lax.all_gather(down_weight, ("batch", "ctx"), axis=0, tiled=True)
    gate_act = rows_product(normed_mid, gate_piece)
    up_act = rows_product(normed_mid, up_piece)
    hidden_f, pull_back = jax.vjp(geglu, gate_act, up_act)
    grad_gate, grad_up = pull_back(rows_product(grad_ffn_b, down_piece))
    grad_gate_b = grad_gate.astype(jnp.bfloat16)
    grad_up_b = grad_up.astype(jnp.bfloat16)
    grad_nm = jnp.dot(grad_gate_b, gate_piece, preferred_element_type=jnp.float32) + jnp.dot(
        grad_up_b, up_piece, preferred_element_type=jnp.float32
    )
    rows_piece = lax.all_gather(normed_mid, ("batch", "ctx"), axis=0, tiled=True)
    cot_piece = lax.all_gather(grad_ffn_b, ("batch", "ctx"), axis=0, tiled=True)
    gate_act = rows_product(rows_piece, gate_weight)
    up_act = rows_product(rows_piece, up_weight)
    hidden_f, pull_back = jax.vjp(geglu, gate_act, up_act)
    grad_gate, grad_up = pull_back(rows_product(cot_piece, down_weight))
    gate_acc = cols_product(grad_gate.astype(jnp.bfloat16), rows_piece)
    up_acc = cols_product(grad_up.astype(jnp.bfloat16), rows_piece)
    down_acc = cols_product(hidden_f.astype(jnp.bfloat16), cot_piece)
    grad_mid_part, grad_three = norm_back(middle, inv_three, gain_three, grad_nm)
    grad_mid = grad_y + grad_mid_part
    grad_branch, grad_two = norm_back(branch, inv_two, gain_two, grad_mid)
    grad_branch_b = grad_branch.astype(jnp.bfloat16)
    out_term = cols_product(attended, grad_branch_b)
    grad_att = rows_product(grad_branch_b, w_out).astype(jnp.bfloat16)
    ga_heads = grad_att.reshape(local_rows, groups, ratio, HEAD_DIM)
    at_heads = attended.reshape(local_rows, groups, ratio, HEAD_DIM)
    delta = jnp.transpose(
        jnp.sum(ga_heads.astype(jnp.float32) * at_heads.astype(jnp.float32), axis=3), (1, 2, 0)
    )
    key_all = kv_all[:, :key_width].reshape(seq_length, groups, HEAD_DIM)
    value_all = kv_all[:, key_width:].reshape(seq_length, groups, HEAD_DIM)
    key_pos = key_positions(block_row, seq_length, local_rows)
    visible = key_pos[None, :] <= query_pos[:, None]
    tanh_val = jnp.tanh(
        jnp.einsum("tgrd,jgd->grtj", q_heads, key_all, preferred_element_type=jnp.float32)
        * scale
        / SOFT_CAP
    )
    prob = jnp.where(visible, jnp.exp(SOFT_CAP * tanh_val) / totals[..., None], 0.0)
    dprob = jnp.einsum("tgrd,jgd->grtj", ga_heads, value_all, preferred_element_type=jnp.float32)
    grad_z = (prob * (dprob - delta[..., None]) * (1.0 - tanh_val * tanh_val) * scale).astype(
        jnp.bfloat16
    )
    grad_query = (
        jnp.einsum("grtj,jgd->tgrd", grad_z, key_all, preferred_element_type=jnp.float32)
        .reshape(local_rows, HEADS * HEAD_DIM)
        .astype(jnp.bfloat16)
    )
    key_terms = jnp.einsum(
        "grtj,tgrd->jgd", grad_z, q_heads, preferred_element_type=jnp.float32
    ).reshape(seq_length, key_width)
    value_terms = jnp.einsum(
        "grtj,tgrd->jgd", prob.astype(jnp.bfloat16), ga_heads, preferred_element_type=jnp.float32
    ).reshape(seq_length, key_width)
    kv_terms = jnp.concatenate((key_terms, value_terms), axis=1)
    kv_own = lax.psum_scatter(kv_terms.astype(jnp.bfloat16), "ctx", scatter_dimension=0, tiled=True)
    grad_keys = kv_own[:, :key_width]
    grad_values = kv_own[:, key_width:]
    query_term = cols_product(normed_in, grad_query)
    key_term = cols_product(normed_in, grad_keys)
    value_term = cols_product(normed_in, grad_values)
    grad_in = (
        rows_product(grad_query, w_query)
        + rows_product(grad_keys, w_key)
        + rows_product(grad_values, w_value)
    )
    grad_x_part, grad_one = norm_back(rows_x, inv_one, gain_one, grad_in)
    input_grad = grad_mid + grad_x_part
    summed = (
        lax.psum_scatter(query_term, ("batch", "ctx"), scatter_dimension=0, tiled=True),
        lax.psum_scatter(key_term, ("batch", "ctx"), scatter_dimension=0, tiled=True),
        lax.psum_scatter(value_term, ("batch", "ctx"), scatter_dimension=0, tiled=True),
        lax.psum_scatter(out_term, ("batch", "ctx"), scatter_dimension=0, tiled=True),
        lax.psum_scatter(grad_one, ("batch", "ctx"), scatter_dimension=0, tiled=True),
        lax.psum_scatter(grad_two, ("batch", "ctx"), scatter_dimension=0, tiled=True),
        lax.psum_scatter(grad_three, ("batch", "ctx"), scatter_dimension=0, tiled=True),
        lax.psum_scatter(grad_four, ("batch", "ctx"), scatter_dimension=0, tiled=True),
    )
    (
        query_grad,
        key_grad,
        value_grad,
        out_grad,
        attn_gain_grad,
        post_attn_gain_grad,
        ffn_gain_grad,
        post_ffn_gain_grad,
    ) = summed
    return (
        output.reshape(1, local_rows, features),
        input_grad.reshape(1, local_rows, features),
        query_grad,
        key_grad,
        value_grad,
        out_grad,
        gate_acc,
        up_acc,
        down_acc,
        attn_gain_grad,
        post_attn_gain_grad,
        ffn_gain_grad,
        post_ffn_gain_grad,
    )


def solution(mesh):
    return jax.shard_map(
        on_device,
        mesh=mesh,
        in_specs=(
            P("batch", "ctx", None),
            P("batch", None),
            P("batch", "ctx", None),
            P(("batch", "ctx")),
            P(("batch", "ctx")),
            P(("batch", "ctx")),
            P(("batch", "ctx")),
            P(("batch", "ctx"), None),
            P(("batch", "ctx"), None),
            P(("batch", "ctx"), None),
            P(("batch", "ctx"), None),
            P(("batch", "ctx"), None),
            P(("batch", "ctx"), None),
            P(("batch", "ctx"), None),
        ),
        out_specs=(
            P("batch", "ctx", None),
            P("batch", "ctx", None),
            P(("batch", "ctx"), None),
            P(("batch", "ctx"), None),
            P(("batch", "ctx"), None),
            P(("batch", "ctx"), None),
            P(("batch", "ctx"), None),
            P(("batch", "ctx"), None),
            P(("batch", "ctx"), None),
            P(("batch", "ctx")),
            P(("batch", "ctx")),
            P(("batch", "ctx")),
            P(("batch", "ctx")),
        ),
        check_vma=False,
    )
```

profile of v0, /device:TPU:0, one launch (start us, length us, event | category | flops | bytes accessed | tf_op | source)
XLA Modules:
  0.0 2215.7 jit_solution(690600870943740185)
XLA Ops:
  12.1 42.5 %all-reduce.9 = (bf16[2304]{0:T(1024)(128)(2,1)S(1)}, bf16[2304]{0:T(1024)(128)(2,1)S(1)}, bf16[2304]{0:T(1024)(128)(2,1)S(1)}, bf16[2304]{0:T(1024)(128)(2,1)S(1)}) all-reduce(bf16[2304]{0:T(1024)(128)(2,1)S(1)} %dynamic-update-slice, bf16[2304]{0:T(1024)(128)(2,1)S(1)} %dynamic-update-slice.1, ...), channel_id=1, replica_groups=mesh['batch'=4,'ctx'=8] {'batch','ctx'}, use_global_device_ids=true, to_apply=%add | all-reduce | flops 9216 | bytes 36864
  58.2 19.2 all-gather.13.cloned.1.call-done
  80.5 61.8 %all-gather.11.cloned.1.call-done = bf16[2304,1024]{1,0:T(8,128)(2,1)} async-done(((bf16[72,1024]{1,0:T(8,128)(2,1)}), bf16[2304,1024]{1,0:T(8,128)(2,1)}) %all-gather.11.cloned.1.call-update) | async-done | bytes 4718608 | tf_op jit(solution)/shard_map/all_gather | solution.py:88
  152.1 39.6 %all-gather.15.cloned.1.call-done = bf16[1024,2048]{1,0:T(8,128)(2,1)} async-done(((bf16[128,2048]{1,0:T(8,128)(2,1)}), bf16[1024,2048]{1,0:T(8,128)(2,1)}) %all-gather.15.cloned.1.call-update) | async-done | bytes 4194320 | tf_op jit(solution)/shard_map/all_gather | solution.py:108
  209.6 65.3 %all-gather.17.cloned.1.call-done = bf16[2304,2048]{1,0:T(8,128)(2,1)} async-done(((bf16[72,2048]{1,0:T(8,128)(2,1)}), bf16[2304,2048]{1,0:T(8,128)(2,1)}) %all-gather.17.cloned.1.call-update) | async-done | bytes 9437200 | tf_op jit(solution)/shard_map/all_gather | solution.py:87
  287.3 70.6 %all-gather.19.cloned.1.call-done = bf16[2048,2304]{1,0:T(8,128)(2,1)} async-done(((bf16[64,2304]{1,0:T(8,128)(2,1)}), bf16[2048,2304]{1,0:T(8,128)(2,1)}) %all-gather.19.cloned.1.call-update) | async-done | bytes 9437200 | tf_op jit(solution)/shard_map/all_gather | solution.py:90
  365.3 231.1 %all-gather.23.cloned.1.call-done = bf16[9216,2304]{1,0:T(8,128)(2,1)} async-done(((bf16[288,2304]{1,0:T(8,128)(2,1)}), bf16[9216,2304]{1,0:T(8,128)(2,1)}) %all-gather.23.cloned.1.call-update) | async-done | bytes 42467344 | tf_op jit(solution)/shard_map/all_gather | solution.py:136
  596.4 22.3 %fusion.117 = f32[128,9216]{1,0:T(8,128)} fusion(bf16[128,2304]{1,0:T(8,128)(2,1)S(1)} %multiply_convert_fusion.11, bf16[9216,2304]{1,0:T(8,128)(2,1)} %all-gather.23.cloned.1.call-done), kind=kOutput, calls=%fused_computation.174 | convolution fusion | flops 5435817984 | bytes 47775744 | tf_op jit(solution)/shard_map/dot_general | solution.py:34
  618.7 215.9 %all-gather.21.cloned.1.call-done = bf16[9216,2304]{1,0:T(8,128)(2,1)} async-done(((bf16[288,2304]{1,0:T(8,128)(2,1)}), bf16[9216,2304]{1,0:T(8,128)(2,1)}) %all-gather.21.cloned.1.call-update) | async-done | bytes 42467344 | tf_op jit(solution)/shard_map/all_gather | solution.py:135
  834.6 22.4 %fusion.116 = f32[128,9216]{1,0:T(8,128)} fusion(bf16[128,2304]{1,0:T(8,128)(2,1)S(1)} %multiply_convert_fusion.11, bf16[9216,2304]{1,0:T(8,128)(2,1)} %all-gather.21.cloned.1.call-done), kind=kOutput, calls=%fused_computation.173 | convolution fusion | flops 5435817984 | bytes 47775744 | tf_op jit(solution)/shard_map/dot_general | solution.py:34
  857.0 215.8 %all-gather.25.cloned.1.call-done = bf16[9216,2304]{1,0:T(8,128)(2,1)} async-done(((bf16[288,2304]{1,0:T(8,128)(2,1)}), bf16[9216,2304]{1,0:T(8,128)(2,1)}) %all-gather.25.cloned.1.call-update) | async-done | bytes 42467344 | tf_op jit(solution)/shard_map/all_gather | solution.py:137
  1072.9 20.8 multiply_reduce_fusion.7
  1099.2 21.7 fusion.118
  1120.9 21.8 fusion.25
  1142.7 25.3 %multiply_reduce_fusion = (f32[2304]{0:T(1024)}, f32[128]{0:T(128)S(1)}, f32[128,2304]{1,0:T(8,128)}) fusion(f32[128,2304]{1,0:T(8,128)S(1)} %get-tuple-element.31, f32[128]{0:T(128)} %copy-done.27, f32[2304]{0:T(1024)S(1)} %convert_element_type.99, f32[128,2304]{1,0:T(8,128)} %fusion.25, bf16[9216,2304]{1,0:T(8,128)(2,1)} %all-gather.23.cloned.1.call-done, ...), kind=kOutput, calls=%fused_computation.82 | convolution fusion | flops 5449676800 | bytes 55462912 | tf_op jit(solution)/shard_map/dot_general | solution.py:155
  1172.6 6.9 convolution_convert_fusion
  1201.3 46.9 %reduce-scatter.16.cloned.1.call-done = bf16[128,2048]{1,0:T(8,128)(2,1)} async-done(((bf16[1024,2048]{1,0:T(8,128)(2,1)}), bf16[128,2048]{1,0:T(8,128)(2,1)}) %reduce-scatter.16.cloned.1.call-update) | async-done | bytes 524304
  1263.4 8.2 fusion.62
  1271.7 8.0 fusion.120
  1279.7 93.9 %all-gather.29.cloned.1.call-done = bf16[4096,2304]{1,0:T(8,128)(2,1)} async-done(((bf16[128,2304]{1,0:T(8,128)(2,1)}), bf16[4096,2304]{1,0:T(8,128)(2,1)}) %all-gather.29.cloned.1.call-update) | async-done | bytes 18874384 | tf_op jit(solution)/shard_map/all_gather | solution.py:158
  1373.5 11.5 fusion.123
  1385.0 12.8 fusion.122
  1405.2 42.1 %all-reduce.8 = (f32[2304]{0:T(1024)}, f32[2304]{0:T(1024)}, f32[2304]{0:T(1024)}, f32[2304]{0:T(1024)}) all-reduce(f32[2304]{0:T(1024)} %get-tuple-element.19, f32[2304]{0:T(1024)} %get-tuple-element.17, f32[2304]{0:T(1024)} %get-tuple-element.15, f32[2304]{0:T(1024)} %get-tuple-element.13), channel_id=7, replica_groups=mesh['batch'=4,'ctx'=8] {'batch','ctx'}, use_global_device_ids=true, to_apply=%region_18.19.clone | all-reduce | flops 9216 | bytes 73728
  1454.4 46.2 %all-gather.27.cloned.1.call-done = bf16[4096,2304]{1,0:T(8,128)(2,1)} async-done(((bf16[128,2304]{1,0:T(8,128)(2,1)}), bf16[4096,2304]{1,0:T(8,128)(2,1)}) %all-gather.27.cloned.1.call-update) | async-done | bytes 18874384 | tf_op jit(solution)/shard_map/all_gather | solution.py:159
  1500.6 13.3 fusion.121
  1513.9 16.9 fusion.21
  1530.8 11.3 fusion.22
  1542.1 21.0 fusion.23
  1563.1 78.3 %reduce-scatter.10.cloned.1.call-done = f32[72,1024]{1,0:T(8,128)} async-done(((f32[2304,1024]{1,0:T(8,128)}), f32[72,1024]{1,0:T(8,128)}) %reduce-scatter.10.cloned.1.call-update) | async-done | bytes 294928 | tf_op jit(solution)/shard_map/reduce_scatter | solution.py:219
  1641.4 141.7 %reduce-scatter.12.cloned.1.call-done = f32[72,1024]{1,0:T(8,128)} async-done(((f32[2304,1024]{1,0:T(8,128)}), f32[72,1024]{1,0:T(8,128)}) %reduce-scatter.12.cloned.1.call-update) | async-done | bytes 294928 | tf_op jit(solution)/shard_map/reduce_scatter | solution.py:220
  1783.0 212.6 %reduce-scatter.8.cloned.1.call-done = f32[72,2048]{1,0:T(8,128)} async-done(((f32[2304,2048]{1,0:T(8,128)}), f32[72,2048]{1,0:T(8,128)}) %reduce-scatter.8.cloned.1.call-update) | async-done | bytes 589840 | tf_op jit(solution)/shard_map/reduce_scatter | solution.py:218
  1995.7 213.0 %reduce-scatter.14.cloned.1.call-done = f32[64,2304]{1,0:T(8,128)} async-done(((f32[2048,2304]{1,0:T(8,128)}), f32[64,2304]{1,0:T(8,128)}) %reduce-scatter.14.cloned.1.call-update) | async-done | bytes 589840 | tf_op jit(solution)/shard_map/reduce_scatter | solution.py:221
  (190 shorter events, 119.5 us)
Async XLA Ops:
  7.2 70.2 %all-gather.13.cloned.1.call-start = ((), (), s32[]{:S(2)}) async-start(), calls=%async_computation.6 | async-start | bytes 4866048 | tf_op jit(solution)/shard_map/all_gather | solution.py:89
  7.9 134.4 %all-gather.11.cloned.1.call-start = ((), (), s32[]{:S(2)}) async-start(), calls=%async_computation.5 | async-start | bytes 4866048 | tf_op jit(solution)/shard_map/all_gather | solution.py:88
  8.7 183.0 %all-gather.15.cloned.1.call-start = ((), (), s32[]{:S(2)}) async-start(), calls=%async_computation.7 | async-start | bytes 4718592 | tf_op jit(solution)/shard_map/all_gather | solution.py:108
  146.4 128.6 %all-gather.17.cloned.1.call-start = ((), (), s32[]{:S(2)}) async-start(), calls=%async_computation.8 | async-start | bytes 9732096 | tf_op jit(solution)/shard_map/all_gather | solution.py:87
  146.9 211.0 %all-gather.19.cloned.1.call-start = ((), (), s32[]{:S(2)}) async-start(), calls=%async_computation.9 | async-start | bytes 9732096 | tf_op jit(solution)/shard_map/all_gather | solution.py:90
  147.5 448.9 %all-gather.23.cloned.1.call-start = ((), (), s32[]{:S(2)}) async-start(), calls=%async_computation.11 | async-start | bytes 43794432 | tf_op jit(solution)/shard_map/all_gather | solution.py:136
  148.1 686.5 %all-gather.21.cloned.1.call-start = ((), (), s32[]{:S(2)}) async-start(), calls=%async_computation.10 | async-start | bytes 43794432 | tf_op jit(solution)/shard_map/all_gather | solution.py:135
  148.8 924.0 %all-gather.25.cloned.1.call-start = ((), (), s32[]{:S(2)}) async-start(), calls=%async_computation.12 | async-start | bytes 43794432 | tf_op jit(solution)/shard_map/all_gather | solution.py:137
  149.6 1098.6 %reduce-scatter.16.cloned.1.call-start = ((), (), s32[]{:S(2)}) async-start(), calls=%async_computation.19 | async-start | bytes 4718592
  149.9 213.4 %copy-start.20 = (f32[2304]{0:T(1024)}, f32[2304]{0:T(1024)S(1)}, u32[]{:S(2)}) copy-start(f32[2304]{0:T(1024)S(1)} %convert_element_type.98) | copy-start | bytes 27652
  152.1 131.7 %copy-start.22 = (pred[128,1024]{0,1:T(8,128)(4,1)}, pred[128,1024]{0,1:T(8,128)(4,1)S(1)}, u32[]{:S(2)}) copy-start(pred[128,1024]{0,1:T(8,128)(4,1)S(1)} %broadcast_compare_fusion) | copy-start | bytes 393220
  287.3 75.9 %copy-start.6 = (bf16[128,4,2,256]{0,3,2,1:T(8,128)(2,1)}, bf16[128,4,2,256]{0,3,2,1:T(8,128)(2,1)S(1)}, u32[]{:S(2)}) copy-start(bf16[128,4,2,256]{0,3,2,1:T(8,128)(2,1)S(1)} %divide_convert_fusion) | copy-start | bytes 1572868
  365.3 469.3 %copy-start.5 = (bf16[128,2304]{1,0:T(8,128)(2,1)}, bf16[128,2304]{1,0:T(8,128)(2,1)S(1)}, u32[]{:S(2)}) copy-start(bf16[128,2304]{1,0:T(8,128)(2,1)S(1)} %multiply_convert_fusion.11) | copy-start | bytes 1769476
  857.0 236.6 %copy-start.24 = (f32[2304]{0:T(1024)S(1)}, f32[2304]{0:T(1024)}, u32[]{:S(2)}) copy-start(f32[2304]{0:T(1024)} %convert_element_type.102) | copy-start | bytes 27652
  1099.2 21.7 copy-start.8
  1142.7 25.3 %copy-start.21 = (f32[2304]{0:T(1024)S(1)}, f32[2304]{0:T(1024)}, u32[]{:S(2)}) copy-start(f32[2304]{0:T(1024)} %copy-done.20) | copy-start | bytes 27652
  1142.7 25.3 %copy-start.28 = (f32[128]{0:T(128)S(1)}, f32[128]{0:T(128)}, u32[]{:S(2)}) copy-start(f32[128]{0:T(128)} %copy-done.27) | copy-start | bytes 1540
  1199.9 173.6 %all-gather.29.cloned.1.call-start = ((), (), s32[]{:S(2)}) async-start(), calls=%async_computation.18 | async-start | bytes 19464192 | tf_op jit(solution)/shard_map/all_gather | solution.py:158
  1200.5 300.1 %all-gather.27.cloned.1.call-start = ((), (), s32[]{:S(2)}) async-start(), calls=%async_computation.17 | async-start | bytes 19464192 | tf_op jit(solution)/shard_map/all_gather | solution.py:159
  1201.2 440.2 %reduce-scatter.10.cloned.1.call-start = ((), (), s32[]{:S(2)}) async-start(), calls=%async_computation.14 | async-start | bytes 9732096 | tf_op jit(solution)/shard_map/reduce_scatter | solution.py:219
  1254.2 528.8 %reduce-scatter.12.cloned.1.call-start = ((), (), s32[]{:S(2)}) async-start(), calls=%async_computation.15 | async-start | bytes 9732096 | tf_op jit(solution)/shard_map/reduce_scatter | solution.py:220
  1260.4 735.3 %reduce-scatter.8.cloned.1.call-start = ((), (), s32[]{:S(2)}) async-start(), calls=%async_computation.13 | async-start | bytes 19464192 | tf_op jit(solution)/shard_map/reduce_scatter | solution.py:218
  1271.6 937.0 %reduce-scatter.14.cloned.1.call-start = ((), (), s32[]{:S(2)}) async-start(), calls=%async_computation.16 | async-start | bytes 19464192 | tf_op jit(solution)/shard_map/reduce_scatter | solution.py:221
  1373.5 24.3 %slice-start = ((s8[9437184]{0:T(1024)(128)(4,1)}), s8[4194304]{0:T(1024)(128)(4,1)S(1)}, s32[]{:S(2)}) async-start(s8[9437184]{0:T(1024)(128)(4,1)} %bitcast.141), calls=%async_computation.20 | async-start | bytes 8388608
  1373.5 24.3 %slice-start.1 = ((s8[9437184]{0:T(1024)(128)(4,1)}), s8[4194304]{0:T(1024)(128)(4,1)S(1)}, s32[]{:S(2)}) async-start(s8[9437184]{0:T(1024)(128)(4,1)} %bitcast.141), calls=%async_computation.21 | async-start | bytes 8388608
  1373.5 27.5 %slice-start.3 = ((s8[4718592]{0:T(1024)(128)(4,1)}), s8[4194304]{0:T(1024)(128)(4,1)S(1)}, s32[]{:S(2)}) async-start(s8[4718592]{0:T(1024)(128)(4,1)} %bitcast.143), calls=%async_computation.23 | async-start | bytes 8388608
  1373.5 29.2 %slice-start.5 = ((s8[4718592]{0:T(1024)(128)(4,1)}), s8[4194304]{0:T(1024)(128)(4,1)S(1)}, s32[]{:S(2)}) async-start(s8[4718592]{0:T(1024)(128)(4,1)} %bitcast.145), calls=%async_computation.25 | async-start | bytes 8388608
  1385.0 17.8 slice-start.6
  1402.8 50.3 %copy-start.4 = (f32[128,2304]{1,0:T(8,128)S(1)}, f32[128,2304]{1,0:T(8,128)}, u32[]{:S(2)}) copy-start(f32[128,2304]{1,0:T(8,128)} %copy-done.3) | copy-start | bytes 3538948
  1500.6 30.2 %slice-start.7 = ((s8[18874368]{0:T(1024)(128)(4,1)}), s8[4194304]{0:T(1024)(128)(4,1)S(1)}, s32[]{:S(2)}) async-start(s8[18874368]{0:T(1024)(128)(4,1)} %bitcast.162), calls=%async_computation.27 | async-start | bytes 8388608
  1500.6 30.2 %slice-start.8 = ((s8[18874368]{0:T(1024)(128)(4,1)}), s8[4194304]{0:T(1024)(128)(4,1)S(1)}, s32[]{:S(2)}) async-start(s8[18874368]{0:T(1024)(128)(4,1)} %bitcast.162), calls=%async_computation.28 | async-start | bytes 8388608
  1500.6 30.2 %slice-start.9 = ((s8[18874368]{0:T(1024)(128)(4,1)}), s8[4194304]{0:T(1024)(128)(4,1)S(1)}, s32[]{:S(2)}) async-start(s8[18874368]{0:T(1024)(128)(4,1)} %bitcast.162), calls=%async_computation.29 | async-start | bytes 8388608
  (29 other events, 161.4 us)
Sparse Core Ops, SparseCore 0:
  11.0 66.3 all-gather.12
  80.4 61.9 all-gather.10
  146.5 45.1 all-gather.14
  194.6 80.3 all-gather.16
  277.8 80.0 all-gather.18
  360.8 235.5 all-gather.22
  599.4 235.1 all-gather.20
  837.6 235.1 all-gather.24
  1200.0 48.0 reduce-scatter.15
  1251.0 122.4 all-gather.28
  1376.6 123.9 all-gather.26
  1506.9 134.4 reduce-scatter.9
  1647.9 135.1 reduce-scatter.11
  1789.9 205.7 reduce-scatter.7
  2002.5 206.0 reduce-scatter.13
where the time goes:
time: 2220 us
  waiting for transfers between devices  1760 us (79%)
  matrix products  294 us (13%)
  blocking collectives  84.6 us (4%)
  local copies, waits for them, and re-layouts  42 us (2%)
    all_gather x1, waiting for transfers between devices, on_device(): up_piece = lax.all_gather(up_weight, ('batch', 'ctx'), axis=0, tiled=True)  231 us
    all_gather x1, waiting for transfers between devices, on_device(): lax.all_gather(gate_weight, ('batch', 'ctx'), axis=0, tiled=True)  216 us
    all_gather x1, waiting for transfers between devices, on_device(): lax.all_gather(down_weight, ('batch', 'ctx'), axis=0, tiled=True)  216 us
    reduce_scatter x1, waiting for transfers between devices, on_device(): lax.psum_scatter(out_term, ('batch', 'ctx'), scatter_dimension=0, tiled=T...  213 us
    reduce_scatter x1, waiting for transfers between devices, on_device(): lax.psum_scatter(query_term, ('batch', 'ctx'), scatter_dimension=0, tiled...  213 us
    reduce_scatter x1, waiting for transfers between devices, on_device(): lax.psum_scatter(value_term, ('batch', 'ctx'), scatter_dimension=0, tiled...  142 us
    dot_general x10, matrix products, rows_product(): lax.dot_general(left_mat, right_mat, (((1,), (1,)), ((), ())), preferred_...  118 us
    all_gather x1, waiting for transfers between devices, on_device(): lax.all_gather(normed_mid, ('batch', 'ctx'), axis=0, tiled=True)  93.9 us
  transfers between devices with their start and end apart: 15, of which 15 were waited for; matrix products, arithmetic and copies ran while one was open for 10% of the time, Pallas kernels for 0%

commit v1 on v0

--- a/solution.py
+++ b/solution.py
@@ -133,8 +133,13 @@
     normed_m, inv_three = normalize(middle, gain_three)
     normed_mid = normed_m.astype(jnp.bfloat16)
     gate_piece = lax.all_gather(gate_weight, ("batch", "ctx"), axis=0, tiled=True)
-    up_piece = lax.all_gather(up_weight, ("batch", "ctx"), axis=0, tiled=True)
-    down_piece = lax.all_gather(down_weight, ("batch", "ctx"), axis=0, tiled=True)
+    up_piece, down_piece = jnp.split(
+        lax.all_gather(
+            jnp.concatenate([up_weight, down_weight], axis=1), ("batch", "ctx"), axis=0, tiled=True
+        ),
+        [up_weight.shape[1]],
+        axis=1,
+    )
     hidden_piece = geglu(
         rows_product(normed_mid, gate_piece), rows_product(normed_mid, up_piece)
     ).astype(jnp.bfloat16)

time: 2220 us -> 2620 us (1.18)
  waiting for transfers between devices: 1760 us -> 2160 us
    all_gather x0 -> x1, waiting for transfers between devices: none -> 419 us  [on_device(): lax.all_gather(jnp.concatenate([up_weight, down_weight], axis=1), ('batch...]
    dot_general x10 -> x9, matrix products: 118 us -> 97.6 us  [rows_product(): lax.dot_general(left_mat, right_mat, (((1,), (1,)), ((), ())), preferred_...]
    unnamed x16 -> x17, waiting for transfers between devices: 52.6 us -> 52.4 us
  transfers between devices with their start and end apart: 15 -> 16, of which waited for: 15 -> 16; matrix products, arithmetic and copies ran while one was open for 10% -> 10% of each run, Pallas kernels for 0% -> 0%
where the time goes in v1:
time: 2620 us
  waiting for transfers between devices  2160 us (82%)
  matrix products  294 us (11%)
  blocking collectives  84.7 us (3%)
  local copies, waits for them, and re-layouts  37.3 us (1%)
    all_gather x1, waiting for transfers between devices, on_device(): lax.all_gather(jnp.concatenate([up_weight, down_weight], axis=1), ('batch...  419 us
    all_gather x1, waiting for transfers between devices, on_device(): lax.all_gather(gate_weight, ('batch', 'ctx'), axis=0, tiled=True)  233 us
    all_gather x1, waiting for transfers between devices, on_device(): up_piece = lax.all_gather(up_weight, ('batch', 'ctx'), axis=0, tiled=True)  216 us
    reduce_scatter x1, waiting for transfers between devices, on_device(): lax.psum_scatter(out_term, ('batch', 'ctx'), scatter_dimension=0, tiled=T...  213 us
    reduce_scatter x1, waiting for transfers between devices, on_device(): lax.psum_scatter(query_term, ('batch', 'ctx'), scatter_dimension=0, tiled...  213 us
    all_gather x1, waiting for transfers between devices, on_device(): lax.all_gather(down_weight, ('batch', 'ctx'), axis=0, tiled=True)  198 us
    reduce_scatter x1, waiting for transfers between devices, on_device(): lax.psum_scatter(value_term, ('batch', 'ctx'), scatter_dimension=0, tiled...  142 us
    dot_general x9, matrix products, rows_product(): lax.dot_general(left_mat, right_mat, (((1,), (1,)), ((), ())), preferred_...  97.6 us
  transfers between devices with their start and end apart: 16, of which 16 were waited for; matrix products, arithmetic and copies ran while one was open for 10% of the time, Pallas kernels for 0%

profile of v1, /device:TPU:0, one launch (start us, length us, event | category | flops | bytes accessed | tf_op | source)
XLA Modules:
  0.0 2617.5 jit_solution(2307980554319169842)
XLA Ops:
  12.1 42.5 %all-reduce.9 = (bf16[2304]{0:T(1024)(128)(2,1)S(1)}, bf16[2304]{0:T(1024)(128)(2,1)S(1)}, bf16[2304]{0:T(1024)(128)(2,1)S(1)}, bf16[2304]{0:T(1024)(128)(2,1)S(1)}) all-reduce(bf16[2304]{0:T(1024)(128)(2,1)S(1)} %dynamic-update-slice, bf16[2304]{0:T(1024)(128)(2,1)S(1)} %dynamic-update-slice.1, ...), channel_id=1, replica_groups=mesh['batch'=4,'ctx'=8] {'batch','ctx'}, use_global_device_ids=true, to_apply=%add | all-reduce | flops 9216 | bytes 36864
  58.2 19.2 all-gather.14.cloned.1.call-done
  80.5 61.8 %all-gather.12.cloned.1.call-done = bf16[2304,1024]{1,0:T(8,128)(2,1)} async-done(((bf16[72,1024]{1,0:T(8,128)(2,1)}), bf16[2304,1024]{1,0:T(8,128)(2,1)}) %all-gather.12.cloned.1.call-update) | async-done | bytes 4718608 | tf_op jit(solution)/shard_map/all_gather | solution.py:88
  153.8 37.8 %all-gather.16.cloned.1.call-done = bf16[1024,2048]{1,0:T(8,128)(2,1)} async-done(((bf16[128,2048]{1,0:T(8,128)(2,1)}), bf16[1024,2048]{1,0:T(8,128)(2,1)}) %all-gather.16.cloned.1.call-update) | async-done | bytes 4194320 | tf_op jit(solution)/shard_map/all_gather | solution.py:108
  207.2 67.8 %all-gather.18.cloned.1.call-done = bf16[2304,2048]{1,0:T(8,128)(2,1)} async-done(((bf16[72,2048]{1,0:T(8,128)(2,1)}), bf16[2304,2048]{1,0:T(8,128)(2,1)}) %all-gather.18.cloned.1.call-update) | async-done | bytes 9437200 | tf_op jit(solution)/shard_map/all_gather | solution.py:87
  285.6 72.3 %all-gather.20.cloned.1.call-done = bf16[2048,2304]{1,0:T(8,128)(2,1)} async-done(((bf16[64,2304]{1,0:T(8,128)(2,1)}), bf16[2048,2304]{1,0:T(8,128)(2,1)}) %all-gather.20.cloned.1.call-update) | async-done | bytes 9437200 | tf_op jit(solution)/shard_map/all_gather | solution.py:90
  363.8 232.5 %all-gather.22.cloned.1.call-done = bf16[9216,2304]{1,0:T(8,128)(2,1)} async-done(((bf16[288,2304]{1,0:T(8,128)(2,1)}), bf16[9216,2304]{1,0:T(8,128)(2,1)}) %all-gather.22.cloned.1.call-update) | async-done | bytes 42467344 | tf_op jit(solution)/shard_map/all_gather | solution.py:135
  596.4 23.7 fusion.123
  620.1 419.2 %all-gather.24.cloned.1.call-done = bf16[9216,4608]{1,0:T(8,128)(2,1)} async-done(((bf16[288,4608]{1,0:T(8,128)(2,1)}), bf16[9216,4608]{1,0:T(8,128)(2,1)}) %all-gather.24.cloned.1.call-update) | async-done | bytes 84934672 | tf_op jit(solution)/shard_map/all_gather | solution.py:137
  1039.3 34.0 %multiply_reduce_fusion.7 = (f32[128]{0:T(128)}, f32[128,2304]{1,0:T(8,128)}) fusion(bf16[9216,4608]{1,0:T(8,128)(2,1)} %all-gather.24.cloned.1.call-done, bf16[128,2304]{1,0:T(8,128)(2,1)} %copy-done.9, f32[128,9216]{1,0:T(8,128)} %fusion.123), kind=kOutput, calls=%fused_computation.95 | convolution fusion | flops 10884022272 | bytes 91423232 | tf_op jit(solution)/shard_map/dot_general | solution.py:146
  1079.1 198.4 %all-gather.26.cloned.1.call-done = bf16[9216,2304]{1,0:T(8,128)(2,1)} async-done(((bf16[288,2304]{1,0:T(8,128)(2,1)}), bf16[9216,2304]{1,0:T(8,128)(2,1)}) %all-gather.26.cloned.1.call-update) | async-done | bytes 42467344 | tf_op jit(solution)/shard_map/all_gather | solution.py:153
  1277.5 22.1 fusion.124
  1299.7 216.1 %all-gather.28.cloned.1.call-done = bf16[9216,2304]{1,0:T(8,128)(2,1)} async-done(((bf16[288,2304]{1,0:T(8,128)(2,1)}), bf16[9216,2304]{1,0:T(8,128)(2,1)}) %all-gather.28.cloned.1.call-update) | async-done | bytes 42467344 | tf_op jit(solution)/shard_map/all_gather | solution.py:152
  1515.8 34.2 %fusion.42 = f32[128,2304]{1,0:T(8,128)} fusion(bf16[9216,2304]{1,0:T(8,128)(2,1)} %all-gather.22.cloned.1.call-done, f32[128,9216]{1,0:T(8,128)} %fusion.123, f32[128,9216]{1,0:T(8,128)} %fusion.124, bf16[128,2304]{1,0:T(8,128)(2,1)} %copy-done.9, bf16[9216,2304]{1,0:T(8,128)(2,1)} %all-gather.28.cloned.1.call-done), kind=kOutput, calls=%fused_computation.60 | convolution fusion | flops 10896408576 | bytes 96141312 | tf_op jit(solution)/shard_map/dot_general | solution.py:160
  1550.0 22.0 multiply_reduce_fusion
  1576.5 6.9 convolution_convert_fusion
  1603.1 46.7 %reduce-scatter.16.cloned.1.call-done = bf16[128,2048]{1,0:T(8,128)(2,1)} async-done(((bf16[1024,2048]{1,0:T(8,128)(2,1)}), bf16[128,2048]{1,0:T(8,128)(2,1)}) %reduce-scatter.16.cloned.1.call-update) | async-done | bytes 524304
  1665.2 8.2 fusion.67
  1673.5 7.7 fusion.126
  1681.3 94.6 %all-gather.32.cloned.1.call-done = bf16[4096,2304]{1,0:T(8,128)(2,1)} async-done(((bf16[128,2304]{1,0:T(8,128)(2,1)}), bf16[4096,2304]{1,0:T(8,128)(2,1)}) %all-gather.32.cloned.1.call-update) | async-done | bytes 18874384 | tf_op jit(solution)/shard_map/all_gather | solution.py:163
  1775.9 11.5 fusion.129
  1787.4 12.9 fusion.128
  1807.7 42.2 %all-reduce.8 = (f32[2304]{0:T(1024)}, f32[2304]{0:T(1024)}, f32[2304]{0:T(1024)}, f32[2304]{0:T(1024)}) all-reduce(f32[2304]{0:T(1024)} %get-tuple-element.19, f32[2304]{0:T(1024)} %get-tuple-element.17, f32[2304]{0:T(1024)} %get-tuple-element.15, f32[2304]{0:T(1024)} %get-tuple-element.13), channel_id=7, replica_groups=mesh['batch'=4,'ctx'=8] {'batch','ctx'}, use_global_device_ids=true, to_apply=%region_18.19.clone | all-reduce | flops 9216 | bytes 73728
  1857.1 45.8 %all-gather.30.cloned.1.call-done = bf16[4096,2304]{1,0:T(8,128)(2,1)} async-done(((bf16[128,2304]{1,0:T(8,128)(2,1)}), bf16[4096,2304]{1,0:T(8,128)(2,1)}) %all-gather.30.cloned.1.call-update) | async-done | bytes 18874384 | tf_op jit(solution)/shard_map/all_gather | solution.py:164
  1902.8 13.2 fusion.127
  1916.1 16.9 fusion.32
  1933.0 11.2 fusion.33
  1944.3 21.0 fusion.34
  1965.3 78.5 %reduce-scatter.10.cloned.1.call-done = f32[72,1024]{1,0:T(8,128)} async-done(((f32[2304,1024]{1,0:T(8,128)}), f32[72,1024]{1,0:T(8,128)}) %reduce-scatter.10.cloned.1.call-update) | async-done | bytes 294928 | tf_op jit(solution)/shard_map/reduce_scatter | solution.py:224
  2043.7 141.5 %reduce-scatter.12.cloned.1.call-done = f32[72,1024]{1,0:T(8,128)} async-done(((f32[2304,1024]{1,0:T(8,128)}), f32[72,1024]{1,0:T(8,128)}) %reduce-scatter.12.cloned.1.call-update) | async-done | bytes 294928 | tf_op jit(solution)/shard_map/reduce_scatter | solution.py:225
  2185.2 212.6 %reduce-scatter.8.cloned.1.call-done = f32[72,2048]{1,0:T(8,128)} async-done(((f32[2304,2048]{1,0:T(8,128)}), f32[72,2048]{1,0:T(8,128)}) %reduce-scatter.8.cloned.1.call-update) | async-done | bytes 589840 | tf_op jit(solution)/shard_map/reduce_scatter | solution.py:223
  2397.9 212.8 %reduce-scatter.14.cloned.1.call-done = f32[64,2304]{1,0:T(8,128)} async-done(((f32[2048,2304]{1,0:T(8,128)}), f32[64,2304]{1,0:T(8,128)}) %reduce-scatter.14.cloned.1.call-update) | async-done | bytes 589840 | tf_op jit(solution)/shard_map/reduce_scatter | solution.py:226
  (195 shorter events, 113.9 us)
Async XLA Ops:
  7.2 70.2 %all-gather.14.cloned.1.call-start = ((), (), s32[]{:S(2)}) async-start(), calls=%async_computation.6 | async-start | bytes 4866048 | tf_op jit(solution)/shard_map/all_gather | solution.py:89
  7.9 134.4 %all-gather.12.cloned.1.call-start = ((), (), s32[]{:S(2)}) async-start(), calls=%async_computation.5 | async-start | bytes 4866048 | tf_op jit(solution)/shard_map/all_gather | solution.py:88
  8.7 183.0 %all-gather.16.cloned.1.call-start = ((), (), s32[]{:S(2)}) async-start(), calls=%async_computation.7 | async-start | bytes 4718592 | tf_op jit(solution)/shard_map/all_gather | solution.py:108
  58.2 216.7 %copy-start.2 = (bf16[128,2304]{1,0:T(8,128)(2,1)}, bf16[128,2304]{1,0:T(8,128)(2,1)S(1)}, u32[]{:S(2)}) copy-start(bf16[128,2304]{1,0:T(8,128)(2,1)S(1)} %multiply_convert_fusion.10) | copy-start | bytes 1769476
  80.5 67.6 %copy-start.10 = (bf16[288,2304]{1,0:T(8,128)(2,1)S(1)}, bf16[288,2304]{1,0:T(8,128)(2,1)}, u32[]{:S(2)}) copy-start(bf16[288,2304]{1,0:T(8,128)(2,1)} %param.26) | copy-start | bytes 3981316
  80.5 67.6 %copy-start.12 = (bf16[288,2304]{1,0:T(8,128)(2,1)S(1)}, bf16[288,2304]{1,0:T(8,128)(2,1)}, u32[]{:S(2)}) copy-start(bf16[288,2304]{1,0:T(8,128)(2,1)} %param.27) | copy-start | bytes 3981316
  146.3 128.6 %all-gather.18.cloned.1.call-start = ((), (), s32[]{:S(2)}) async-start(), calls=%async_computation.8 | async-start | bytes 9732096 | tf_op jit(solution)/shard_map/all_gather | solution.py:87
  146.9 211.0 %all-gather.20.cloned.1.call-start = ((), (), s32[]{:S(2)}) async-start(), calls=%async_computation.9 | async-start | bytes 9732096 | tf_op jit(solution)/shard_map/all_gather | solution.py:90
  147.5 448.9 %all-gather.22.cloned.1.call-start = ((), (), s32[]{:S(2)}) async-start(), calls=%async_computation.10 | async-start | bytes 43794432 | tf_op jit(solution)/shard_map/all_gather | solution.py:135
  148.1 891.2 %all-gather.24.cloned.1.call-start = ((), (), s32[]{:S(2)}) async-start(), calls=%async_computation.11 | async-start | bytes 87588864 | tf_op jit(solution)/shard_map/all_gather | solution.py:137
  149.9 1127.7 %all-gather.26.cloned.1.call-start = ((), (), s32[]{:S(2)}) async-start(), calls=%async_computation.12 | async-start | bytes 43794432 | tf_op jit(solution)/shard_map/all_gather | solution.py:153
  150.6 1365.2 %all-gather.28.cloned.1.call-start = ((), (), s32[]{:S(2)}) async-start(), calls=%async_computation.13 | async-start | bytes 43794432 | tf_op jit(solution)/shard_map/all_gather | solution.py:152
  151.4 1498.4 %reduce-scatter.16.cloned.1.call-start = ((), (), s32[]{:S(2)}) async-start(), calls=%async_computation.20 | async-start | bytes 4718592
  151.6 211.6 %copy-start.23 = (f32[2304]{0:T(1024)}, f32[2304]{0:T(1024)S(1)}, u32[]{:S(2)}) copy-start(f32[2304]{0:T(1024)S(1)} %convert_element_type.98) | copy-start | bytes 27652
  153.8 128.1 %copy-start.25 = (pred[128,1024]{0,1:T(8,128)(4,1)}, pred[128,1024]{0,1:T(8,128)(4,1)S(1)}, u32[]{:S(2)}) copy-start(pred[128,1024]{0,1:T(8,128)(4,1)S(1)} %broadcast_compare_fusion) | copy-start | bytes 393220
  207.2 73.1 %copy-start.16 = (bf16[1024,4,256,1]{0,2,3,1:T(8,128)(2,1)S(1)}, bf16[1024,4,256,1]{0,2,3,1:T(8,128)(2,1)}, u32[]{:S(2)}) copy-start(bf16[1024,4,256,1]{0,2,3,1:T(8,128)(2,1)} %copy.68) | copy-start | bytes 6291460
  285.6 77.6 %copy-start.7 = (bf16[128,4,2,256]{0,3,2,1:T(8,128)(2,1)}, bf16[128,4,2,256]{0,3,2,1:T(8,128)(2,1)S(1)}, u32[]{:S(2)}) copy-start(bf16[128,4,2,256]{0,3,2,1:T(8,128)(2,1)S(1)} %divide_convert_fusion) | copy-start | bytes 1572868
  363.6 232.7 %copy-start.29 = (f32[128]{0:T(128)}, f32[128]{0:T(128)S(1)}, u32[]{:S(2)}) copy-start(f32[128]{0:T(128)S(1)} %add_rsqrt_fusion.1) | copy-start | bytes 1540
  363.8 232.6 %copy-start.9 = (bf16[128,2304]{1,0:T(8,128)(2,1)}, bf16[128,2304]{1,0:T(8,128)(2,1)S(1)}, u32[]{:S(2)}) copy-start(bf16[128,2304]{1,0:T(8,128)(2,1)S(1)} %multiply_convert_fusion.9) | copy-start | bytes 1769476
  620.0 454.0 %copy-start.4 = (f32[1,128,2304]{2,1,0:T(8,128)S(1)}, f32[1,128,2304]{2,1,0:T(8,128)}, u32[]{:S(2)}) copy-start(f32[1,128,2304]{2,1,0:T(8,128)} %param.16) | copy-start | bytes 3538948
  1601.5 48.3 %copy-start.3 = (bf16[128,2304]{1,0:T(8,128)(2,1)S(1)}, bf16[128,2304]{1,0:T(8,128)(2,1)}, u32[]{:S(2)}) copy-start(bf16[128,2304]{1,0:T(8,128)(2,1)} %copy-done.2) | copy-start | bytes 1769476
  1601.6 174.3 %all-gather.32.cloned.1.call-start = ((), (), s32[]{:S(2)}) async-start(), calls=%async_computation.19 | async-start | bytes 19464192 | tf_op jit(solution)/shard_map/all_gather | solution.py:163
  1602.3 300.5 %all-gather.30.cloned.1.call-start = ((), (), s32[]{:S(2)}) async-start(), calls=%async_computation.18 | async-start | bytes 19464192 | tf_op jit(solution)/shard_map/all_gather | solution.py:164
  1602.9 440.9 %reduce-scatter.10.cloned.1.call-start = ((), (), s32[]{:S(2)}) async-start(), calls=%async_computation.15 | async-start | bytes 9732096 | tf_op jit(solution)/shard_map/reduce_scatter | solution.py:224
  1655.9 529.4 %reduce-scatter.12.cloned.1.call-start = ((), (), s32[]{:S(2)}) async-start(), calls=%async_computation.16 | async-start | bytes 9732096 | tf_op jit(solution)/shard_map/reduce_scatter | solution.py:225
  1662.1 735.8 %reduce-scatter.8.cloned.1.call-start = ((), (), s32[]{:S(2)}) async-start(), calls=%async_computation.14 | async-start | bytes 19464192 | tf_op jit(solution)/shard_map/reduce_scatter | solution.py:223
  1673.5 937.3 %reduce-scatter.14.cloned.1.call-start = ((), (), s32[]{:S(2)}) async-start(), calls=%async_computation.17 | async-start | bytes 19464192 | tf_op jit(solution)/shard_map/reduce_scatter | solution.py:226
  1681.3 106.1 %copy-start.11 = (bf16[288,2304]{1,0:T(8,128)(2,1)S(1)}, bf16[288,2304]{1,0:T(8,128)(2,1)}, u32[]{:S(2)}) copy-start(bf16[288,2304]{1,0:T(8,128)(2,1)} %param.26) | copy-start | bytes 3981316
  1805.2 50.5 %copy-start.6 = (f32[128,2304]{1,0:T(8,128)S(1)}, f32[128,2304]{1,0:T(8,128)}, u32[]{:S(2)}) copy-start(f32[128,2304]{1,0:T(8,128)} %copy-done.5) | copy-start | bytes 3538948
  1902.8 30.1 %slice-start.7 = ((s8[18874368]{0:T(1024)(128)(4,1)}), s8[4194304]{0:T(1024)(128)(4,1)S(1)}, s32[]{:S(2)}) async-start(s8[18874368]{0:T(1024)(128)(4,1)} %bitcast.162), calls=%async_computation.28 | async-start | bytes 8388608
  1902.8 30.1 %slice-start.8 = ((s8[18874368]{0:T(1024)(128)(4,1)}), s8[4194304]{0:T(1024)(128)(4,1)S(1)}, s32[]{:S(2)}) async-start(s8[18874368]{0:T(1024)(128)(4,1)} %bitcast.162), calls=%async_computation.29 | async-start | bytes 8388608
  1902.8 30.1 %slice-start.9 = ((s8[18874368]{0:T(1024)(128)(4,1)}), s8[4194304]{0:T(1024)(128)(4,1)S(1)}, s32[]{:S(2)}) async-start(s8[18874368]{0:T(1024)(128)(4,1)} %bitcast.162), calls=%async_computation.30 | async-start | bytes 8388608
  (31 other events, 262.5 us)
Sparse Core Ops, SparseCore 0:
  11.0 66.3 all-gather.13
  80.4 61.9 all-gather.11
  146.5 45.1 all-gather.15
  194.5 80.3 all-gather.17
  277.8 80.0 all-gather.19
  360.8 235.5 all-gather.21
  600.0 439.2 all-gather.23
  1042.3 235.1 all-gather.25
  1280.6 235.1 all-gather.27
  1601.7 48.0 reduce-scatter.15
  1653.4 122.4 all-gather.31
  1778.8 123.9 all-gather.29
  1909.3 134.4 reduce-scatter.9
  2050.1 135.1 reduce-scatter.11
  2192.1 205.7 reduce-scatter.7
  2404.7 205.9 reduce-scatter.13
